TPU v7x, 32 devices: a whole 2x2x4 slice. The times are simulated.
32 devices in a mesh: groups: 2 (over y), space: 4 (over x, core), chan: 4 (over z).
Axes of the slice: x: 2, y: 2, z: 4, core: 2. Of those that a mesh axis runs over, the one named last changes fastest.
Arguments:
- volume: bfloat16 [32, 16, 256, 256], P(('groups', 'space'), 'chan'), parts along dimension 0, may hold values from -6 to 6
- weight: bfloat16 [8, 256, 256], P(None, 'space', 'chan'), may hold values from -0.125 to 0.125
- cotangent: bfloat16 [16, 8, 128, 256], P(('groups', 'space'), None, None, 'chan'), parts along dimension 0, may hold values from -6 to 6
Outputs:
- grad_volume: bfloat16 [32, 16, 256, 256], P(('groups', 'space'), 'chan'), parts along dimension 0
- grad_weight: float32 [16, 256, 256], P('groups', 'space', 'chan'), parts along dimension 0
There are 2 independent parts, one for each index of `groups`. A program takes and returns all parts, laid end to end along the dimension named above; an argument that names none is the same for every part. Nothing has to cross between parts.
All inputs are finite; a program needn't handle non-finite values.
Results may differ from a plain program's by a relative error of at most 0.0049.
Values may be sent and summed in bfloat16 or wider, within the bound.
A program may use at most 64 MiB of HBM per device.

v0:
```python
import jax
import jax.numpy as jnp
from jax import lax
from jax.sharding import PartitionSpec as P


def patch_rows(block):
    cells_x, cells_y, cells_z, in_chan = block.shape
    shaped = block.reshape(cells_x // 2, 2, cells_y // 2, 2, cells_z // 2, 2, in_chan)
    return shaped.transpose(0, 2, 4, 1, 3, 5, 6).reshape(-1, 8, in_chan)


def unpatch(rows, cells_x, cells_y, cells_z):
    in_chan = rows.shape[2]
    shaped = rows.reshape(cells_x // 2, cells_y // 2, cells_z // 2, 2, 2, 2, in_chan)
    return shaped.transpose(0, 3, 1, 4, 2, 5, 6).reshape(cells_x, cells_y, cells_z, in_chan)


def shards(volume, weight, cotangent):
    cells_x, cells_y, cells_z, in_chan = volume.shape
    patches = patch_rows(volume)
    out_rows = patches.shape[0]
    wide_w = lax.all_gather(weight, "chan", axis=2, tiled=True)
    cot_tiles = lax.all_to_all(cotangent, "chan", split_axis=1, concat_axis=3, tiled=True)
    out_chan = cot_tiles.shape[3]
    upstream = cot_tiles.reshape(out_rows, out_chan)
    whole_w = lax.all_gather(wide_w, "space", axis=1, tiled=True)
    pre_act = jnp.einsum("mkc,kco->mo", patches, whole_w, preferred_element_type=jnp.float32)
    squash = jax.nn.sigmoid(pre_act)
    slopes = squash * (1.0 + pre_act * (1.0 - squash))
    deltas = (upstream.astype(jnp.float32) * slopes).astype(jnp.bfloat16)
    grad_rows = jnp.einsum(
        "mo,kco->mkc", deltas, whole_w, preferred_element_type=jnp.float32
    ).astype(jnp.bfloat16)
    grad_volume = unpatch(grad_rows, cells_x, cells_y, cells_z)
    partial_w = jnp.einsum("mkc,mo->kco", patches, deltas, preferred_element_type=jnp.float32)
    by_chan = lax.psum_scatter(partial_w, "chan", scatter_dimension=2, tiled=True)
    owned_sum = lax.psum_scatter(by_chan, "space", scatter_dimension=1, tiled=True)
    grad_weight = owned_sum / out_rows
    return (grad_volume, grad_weight)


def solution(mesh):
    return jax.shard_map(
        shards,
        mesh=mesh,
        in_specs=(
            P(("groups", "space"), "chan", None, None),
            P(None, "space", "chan"),
            P(("groups", "space"), None, None, "chan"),
        ),
        out_specs=(P(("groups", "space"), "chan", None, None), P("groups", "space", "chan")),
        check_vma=False,
    )
```

profile of v0, /device:TPU:0, one launch (start us, length us, event | category | flops | bytes accessed | tf_op | source)
XLA Modules:
  0.0 125.6 jit_solution(15146380185082460627)
XLA Ops:
  7.2 0.0 copy-start.2
  7.2 0.0 copy-start
  7.2 0.0 all-gather.2.cloned.1.call-start
  7.2 1.2 copy.19
  8.4 17.4 %all_gather.6 = bf16[8,64,256]{1,0,2:T(8,128)(2,1)S(1)} all-gather(bf16[8,64,64]{1,0,2:T(8,128)(2,1)S(1)} %copy.19), channel_id=1, replica_groups=mesh['groups'=2,'space'=4,'chan'=4] {'chan'}, dimensions={2}, use_global_device_ids=true | all-gather | bytes 327680 | tf_op jit(solution)/shard_map/all_gather | solution.py:23
  25.8 1.0 copy.20
  26.8 0.0 all-gather.2.cloned.1.call-update
  26.9 0.0 copy-done.2
  26.9 0.7 copy.16
  27.6 5.4 %all-to-all-start = ((bf16[2,8,128,64]{2,3,0,1:T(8,128)(2,1)}), bf16[2,8,128,64]{2,3,0,1:T(8,128)(2,1)S(1)}, u32[]{:S(2)}, u32[]{:S(2)}) async-start(bf16[2,8,128,64]{2,3,0,1:T(8,128)(2,1)} %copy.16), calls=%async_computation | async-start | bytes 524288 | tf_op jit(solution)/shard_map/all_to_all | solution.py:24
  33.0 2.2 %reshape.22 = bf16[2,2,2,2,128,2,256]{6,5,4,3,2,1,0:T(2,128)(2,1)} reshape(bf16[4,4,256,256]{3,2,1,0:T(8,128)(2,1)S(1)} %copy-done) | data formatting | bytes 4194304 | tf_op jit(solution)/shard_map/reshape | solution.py:9
  35.2 2.1 %copy.18 = bf16[2,2,128,2,2,2,256]{6,2,1,0,5,4,3:T(8,128)(2,1)S(1)} copy(bf16[2,2,128,2,2,2,256]{6,5,2,4,1,3,0:T(2,128)(2,1)} %bitcast.37) | data formatting | bytes 4194304 | tf_op jit(solution)/shard_map/transpose | solution.py:10
  37.3 2.4 %all-to-all-done = bf16[2,8,128,64]{2,3,0,1:T(8,128)(2,1)S(1)} async-done(((bf16[2,8,128,64]{2,3,0,1:T(8,128)(2,1)}), bf16[2,8,128,64]{2,3,0,1:T(8,128)(2,1)S(1)}, u32[]{:S(2)}, u32[]{:S(2)}) %all-to-all-start) | async-done | bytes 262176 | tf_op jit(solution)/shard_map/all_to_all | solution.py:24
  39.8 0.3 copy.30
  40.0 0.4 reshape.26
  40.5 1.0 copy.21
  41.4 4.0 %all-gather.2.cloned.1.call-done = bf16[8,256,256]{2,1,0:T(8,128)(2,1)} async-done(((bf16[8,64,256]{2,1,0:T(8,128)(2,1)}), bf16[8,256,256]{2,1,0:T(8,128)(2,1)}) %all-gather.2.cloned.1.call-update) | async-done | bytes 1048592 | tf_op jit(solution)/shard_map/all_gather | solution.py:27
  45.5 2.1 %fusion = bf16[512,256,1]{1,0,2:T(8,128)(2,1)S(1)} fusion(f32[512,256]{1,0:T(8,128)} %copy.21, bf16[512,8,256]{2,0,1:T(8,128)(2,1)S(1)} %bitcast.34, bf16[8,256,256]{2,1,0:T(8,128)(2,1)} %all-gather.2.cloned.1.call-done), kind=kOutput, calls=%fused_computation.5 | convolution fusion | flops 538050560 | bytes 3932160 | tf_op jit(solution)/shard_map/mkc,kco->mo/dot_general | solution.py:28
  47.6 2.0 %convolution_bitcast_fusion = f32[8,256,256]{1,2,0:T(8,128)} fusion(bf16[512,256,1]{1,0,2:T(8,128)(2,1)S(1)} %fusion, bf16[512,8,256]{2,0,1:T(8,128)(2,1)S(1)} %bitcast.35), kind=kOutput, calls=%fused_computation.1 | convolution fusion | flops 536870912 | bytes 4456448 | tf_op jit(solution)/shard_map/mkc,mo->kco/dot_general | solution.py:36
  49.7 0.0 reduce-scatter.5.cloned.1.call-update
  49.7 0.0 reduce-scatter.7.cloned.1.call-start
  49.7 43.7 %reduce-scatter.5.cloned.1.call-done = f32[8,256,64]{1,2,0:T(8,128)} async-done(((f32[8,256,256]{1,2,0:T(8,128)}), f32[8,256,64]{1,2,0:T(8,128)}) %reduce-scatter.5.cloned.1.call-update) | async-done | bytes 524304 | tf_op jit(solution)/shard_map/reduce_scatter | solution.py:37
  93.5 1.5 %copy.27 = f32[8,256,64]{2,0,1:T(8,128)S(1)} copy(f32[8,256,64]{1,2,0:T(8,128)} %reduce-scatter.5.cloned.1.call-done) | data formatting | bytes 1048576
  95.0 1.1 reshape.31
  96.0 0.0 reduce-scatter.7.cloned.1.call-update
  96.1 0.7 convolution_convert_fusion
  96.8 2.2 %copy.22 = bf16[2,2,2,2,128,2,256]{6,5,4,3,2,1,0:T(2,128)(2,1)S(1)} copy(bf16[2,2,2,2,128,2,256]{6,4,2,0,5,3,1:T(8,128)(2,1)S(1)} %bitcast.36) | data formatting | bytes 4194304 | tf_op jit(solution)/shard_map/transpose | solution.py:16
  99.0 2.2 %reshape.25 = bf16[4,4,256,256]{3,2,1,0:T(8,128)(2,1)} reshape(bf16[2,2,2,2,128,2,256]{6,5,4,3,2,1,0:T(2,128)(2,1)S(1)} %copy.22) | data formatting | bytes 4194304 | tf_op jit(solution)/shard_map/reshape | solution.py:16
  101.2 15.9 %reduce-scatter.7.cloned.1.call-done = f32[64,512]{1,0:T(8,128)} async-done(((f32[256,512]{1,0:T(8,128)}), f32[64,512]{1,0:T(8,128)}) %reduce-scatter.7.cloned.1.call-update) | async-done | bytes 131088
  117.1 1.0 reshape.32
  118.1 0.1 copy.28
  118.2 0.8 copy.24
  (5 shorter events, 0.0 us)
Async XLA Ops:
  7.2 19.7 %copy-start.2 = (bf16[2,8,128,64]{2,3,1,0:T(8,128)(2,1)S(1)}, bf16[2,8,128,64]{2,3,1,0:T(8,128)(2,1)}, u32[]{:S(2)}) copy-start(bf16[2,8,128,64]{2,3,1,0:T(8,128)(2,1)} %param.5) | copy-start | bytes 786436
  7.2 25.8 %copy-start = (bf16[4,4,256,256]{3,2,1,0:T(8,128)(2,1)S(1)}, bf16[4,4,256,256]{3,2,1,0:T(8,128)(2,1)}, u32[]{:S(2)}) copy-start(bf16[4,4,256,256]{3,2,1,0:T(8,128)(2,1)} %param.3) | copy-start | bytes 6291460
  7.2 38.3 %all-gather.2.cloned.1.call-start = ((), (), s32[]{:S(2)}) async-start(), calls=%async_computation.3 | async-start | bytes 1310720 | tf_op jit(solution)/shard_map/all_gather | solution.py:27
  27.6 12.2 %all-to-all-start = ((bf16[2,8,128,64]{2,3,0,1:T(8,128)(2,1)}), bf16[2,8,128,64]{2,3,0,1:T(8,128)(2,1)S(1)}, u32[]{:S(2)}, u32[]{:S(2)}) async-start(bf16[2,8,128,64]{2,3,0,1:T(8,128)(2,1)} %copy.16), calls=%async_computation | async-start | bytes 524288 | tf_op jit(solution)/shard_map/all_to_all | solution.py:24
  33.0 60.5 %reduce-scatter.5.cloned.1.call-start = ((), (), s32[]{:S(2)}) async-start(), calls=%async_computation.4 | async-start | bytes 2621440 | tf_op jit(solution)/shard_map/reduce_scatter | solution.py:37
  49.7 46.4 %copy-start.1 = (bf16[8,256,256]{2,1,0:T(8,128)(2,1)S(1)}, bf16[8,256,256]{2,1,0:T(8,128)(2,1)}, u32[]{:S(2)}) copy-start(bf16[8,256,256]{2,1,0:T(8,128)(2,1)} %all-gather.2.cloned.1.call-done) | copy-start | bytes 3145732
  49.7 67.4 %reduce-scatter.7.cloned.1.call-start = ((), (), s32[]{:S(2)}) async-start(), calls=%async_computation.5 | async-start | bytes 655360
Sparse Core Ops, SparseCore 0:
  27.0 18.4 all-gather.1
  49.8 43.6 reduce-scatter.4
  96.2 20.8 reduce-scatter.6
where the time goes:
time: 126 us
  waiting for transfers between devices  66.1 us (52%)
  local copies, waits for them, and re-layouts  17.9 us (14%)
  blocking collectives  17.4 us (14%)
  between operations  13.9 us (11%)
  starting transfers between devices  5.47 us (4%)
  matrix products  4.93 us (4%)
    reduce_scatter x1, waiting for transfers between devices, shards(): lax.psum_scatter(partial_w, 'chan', scatter_dimension=2, tiled=True)  43.7 us
    all_gather x1, blocking collectives, shards(): wide_w = lax.all_gather(weight, 'chan', axis=2, tiled=True)  17.4 us
    unnamed x4, waiting for transfers between devices  15.9 us
    unnamed x13, local copies, waits for them, and re-layouts  6.45 us
    all_to_all x1, starting transfers between devices, shards(): lax.all_to_all(cotangent, 'chan', split_axis=1, concat_axis=3, tiled=True)  5.38 us
    all_gather x1, waiting for transfers between devices, shards(): whole_w = lax.all_gather(wide_w, 'space', axis=1, tiled=True)  4.02 us
  transfers between devices with their start and end apart: 4, of which 4 were waited for; matrix products, arithmetic and copies ran while one was open for 9% of the time, Pallas kernels for 0%

commit v1 on v0

--- a/solution.py
+++ b/solution.py
@@ -24,7 +24,7 @@
     cot_tiles = lax.all_to_all(cotangent, "chan", split_axis=1, concat_axis=3, tiled=True)
     out_chan = cot_tiles.shape[3]
     upstream = cot_tiles.reshape(out_rows, out_chan)
-    whole_w = lax.all_gather(wide_w, "space", axis=1, tiled=True)
+    whole_w = jnp.concatenate(lax.all_gather(wide_w, "space"), axis=1)
     pre_act = jnp.einsum("mkc,kco->mo", patches, whole_w, preferred_element_type=jnp.float32)
     squash = jax.nn.sigmoid(pre_act)
     slopes = squash * (1.0 + pre_act * (1.0 - squash))

time: 126 us -> 126 us (level)
  matrix products: 4.93 us -> 3.57 us
  local copies, waits for them, and re-layouts: 17.9 us -> 19.2 us
    dot_general x1, matrix products: 2.13 us -> 0.78 us  [shards(): jnp.einsum('mkc,kco->mo', patches, whole_w, preferred_element_type=jnp.fl...]
    all_gather x0 -> x1, local copies, waits for them, and re-layouts: none -> 1.35 us  [shards(): whole_w = jnp.concatenate(lax.all_gather(wide_w, 'space'), axis=1)]
where the time goes in v1:
time: 126 us
  waiting for transfers between devices  66.1 us (52%)
  local copies, waits for them, and re-layouts  19.2 us (15%)
  blocking collectives  17.4 us (14%)
  between operations  13.8 us (11%)
  starting transfers between devices  5.47 us (4%)
  matrix products  3.57 us (3%)
    reduce_scatter x1, waiting for transfers between devices, shards(): lax.psum_scatter(partial_w, 'chan', scatter_dimension=2, tiled=True)  43.7 us
    all_gather x1, blocking collectives, shards(): wide_w = lax.all_gather(weight, 'chan', axis=2, tiled=True)  17.4 us
    unnamed x4, waiting for transfers between devices  15.9 us
    unnamed x13, local copies, waits for them, and re-layouts  6.44 us
    all_to_all x1, starting transfers between devices, shards(): lax.all_to_all(cotangent, 'chan', split_axis=1, concat_axis=3, tiled=True)  5.38 us
    all_gather x1, waiting for transfers between devices, shards(): whole_w = jnp.concatenate(lax.all_gather(wide_w, 'space'), axis=1)  4.02 us
  transfers between devices with their start and end apart: 4, of which 4 were waited for; matrix products, arithmetic and copies ran while one was open for 9% of the time, Pallas kernels for 0%

profile of v1, /device:TPU:0, one launch (start us, length us, event | category | flops | bytes accessed | tf_op | source)
XLA Modules:
  0.0 125.6 jit_solution(16790328148949751141)
XLA Ops:
  7.2 0.0 copy-start.2
  7.2 0.0 copy-start
  7.2 0.0 all-gather.3.cloned.1.call-start
  7.2 1.2 copy.21
  8.4 17.4 %all_gather.9 = bf16[8,64,256]{1,0,2:T(8,128)(2,1)S(1)} all-gather(bf16[8,64,64]{1,0,2:T(8,128)(2,1)S(1)} %copy.21), channel_id=1, replica_groups=mesh['groups'=2,'space'=4,'chan'=4] {'chan'}, dimensions={2}, use_global_device_ids=true | all-gather | bytes 327680 | tf_op jit(solution)/shard_map/all_gather | solution.py:23
  25.8 1.0 copy.22
  26.8 0.0 all-gather.3.cloned.1.call-update
  26.9 0.7 copy.18
  27.6 5.4 %all-to-all-start = ((bf16[2,8,128,64]{2,3,0,1:T(8,128)(2,1)}), bf16[2,8,128,64]{2,3,0,1:T(8,128)(2,1)S(1)}, u32[]{:S(2)}, u32[]{:S(2)}) async-start(bf16[2,8,128,64]{2,3,0,1:T(8,128)(2,1)} %copy.18), calls=%async_computation | async-start | bytes 524288 | tf_op jit(solution)/shard_map/all_to_all | solution.py:24
  33.0 2.2 %reshape.28 = bf16[2,2,2,2,128,2,256]{6,5,4,3,2,1,0:T(2,128)(2,1)} reshape(bf16[4,4,256,256]{3,2,1,0:T(8,128)(2,1)S(1)} %copy-done) | data formatting | bytes 4194304 | tf_op jit(solution)/shard_map/reshape | solution.py:9
  35.2 2.1 %copy.20 = bf16[2,2,128,2,2,2,256]{6,2,1,0,5,4,3:T(8,128)(2,1)S(1)} copy(bf16[2,2,128,2,2,2,256]{6,5,2,4,1,3,0:T(2,128)(2,1)} %bitcast.41) | data formatting | bytes 4194304 | tf_op jit(solution)/shard_map/transpose | solution.py:10
  37.3 2.4 %all-to-all-done = bf16[2,8,128,64]{2,3,0,1:T(8,128)(2,1)S(1)} async-done(((bf16[2,8,128,64]{2,3,0,1:T(8,128)(2,1)}), bf16[2,8,128,64]{2,3,0,1:T(8,128)(2,1)S(1)}, u32[]{:S(2)}, u32[]{:S(2)}) %all-to-all-start) | async-done | bytes 262176 | tf_op jit(solution)/shard_map/all_to_all | solution.py:24
  39.8 0.3 copy.33
  40.0 0.4 reshape.34
  40.5 1.0 copy.24
  41.4 4.0 %all-gather.3.cloned.1.call-done = bf16[32,64,256]{2,1,0:T(8,128)(2,1)} async-done(((bf16[8,64,256]{2,1,0:T(8,128)(2,1)}), bf16[32,64,256]{2,1,0:T(8,128)(2,1)}) %all-gather.3.cloned.1.call-update) | async-done | bytes 1048592 | tf_op jit(solution)/shard_map/all_gather | solution.py:27
  45.5 1.4 %copy.23 = bf16[4,8,64,256]{3,2,0,1:T(8,128)(2,1)S(1)} copy(bf16[4,8,64,256]{3,2,1,0:T(8,128)(2,1)} %bitcast.47) | data formatting | bytes 2097152 | tf_op jit(solution)/shard_map/all_gather | solution.py:27
  46.8 0.8 fusion
  47.6 2.0 %convolution_bitcast_fusion = f32[8,256,256]{1,2,0:T(8,128)} fusion(bf16[512,256,1]{1,0,2:T(8,128)(2,1)S(1)} %fusion, bf16[512,8,256]{2,0,1:T(8,128)(2,1)S(1)} %bitcast.39), kind=kOutput, calls=%fused_computation.1 | convolution fusion | flops 536870912 | bytes 4456448 | tf_op jit(solution)/shard_map/mkc,mo->kco/dot_general | solution.py:36
  49.7 0.0 reduce-scatter.5.cloned.1.call-update
  49.7 0.0 reduce-scatter.7.cloned.1.call-start
  49.7 43.7 %reduce-scatter.5.cloned.1.call-done = f32[8,256,64]{1,2,0:T(8,128)} async-done(((f32[8,256,256]{1,2,0:T(8,128)}), f32[8,256,64]{1,2,0:T(8,128)}) %reduce-scatter.5.cloned.1.call-update) | async-done | bytes 524304 | tf_op jit(solution)/shard_map/reduce_scatter | solution.py:37
  93.5 1.5 %copy.30 = f32[8,256,64]{2,0,1:T(8,128)S(1)} copy(f32[8,256,64]{1,2,0:T(8,128)} %reduce-scatter.5.cloned.1.call-done) | data formatting | bytes 1048576
  95.0 1.1 reshape.40
  96.0 0.0 reduce-scatter.7.cloned.1.call-update
  96.1 0.7 convolution_convert_fusion
  96.8 2.2 %copy.25 = bf16[2,2,2,2,128,2,256]{6,5,4,3,2,1,0:T(2,128)(2,1)S(1)} copy(bf16[2,2,2,2,128,2,256]{6,4,2,0,5,3,1:T(8,128)(2,1)S(1)} %bitcast.40) | data formatting | bytes 4194304 | tf_op jit(solution)/shard_map/transpose | solution.py:16
  99.0 2.2 %reshape.33 = bf16[4,4,256,256]{3,2,1,0:T(8,128)(2,1)} reshape(bf16[2,2,2,2,128,2,256]{6,5,4,3,2,1,0:T(2,128)(2,1)S(1)} %copy.25) | data formatting | bytes 4194304 | tf_op jit(solution)/shard_map/reshape | solution.py:16
  101.2 15.8 %reduce-scatter.7.cloned.1.call-done = f32[64,512]{1,0:T(8,128)} async-done(((f32[256,512]{1,0:T(8,128)}), f32[64,512]{1,0:T(8,128)}) %reduce-scatter.7.cloned.1.call-update) | async-done | bytes 131088
  117.0 1.0 reshape.41
  118.0 0.1 copy.31
  118.2 0.8 copy.27
  (6 shorter events, 0.0 us)
Async XLA Ops:
  7.2 19.7 %copy-start.2 = (bf16[2,8,128,64]{2,3,1,0:T(8,128)(2,1)S(1)}, bf16[2,8,128,64]{2,3,1,0:T(8,128)(2,1)}, u32[]{:S(2)}) copy-start(bf16[2,8,128,64]{2,3,1,0:T(8,128)(2,1)} %param.5) | copy-start | bytes 786436
  7.2 25.8 %copy-start = (bf16[4,4,256,256]{3,2,1,0:T(8,128)(2,1)S(1)}, bf16[4,4,256,256]{3,2,1,0:T(8,128)(2,1)}, u32[]{:S(2)}) copy-start(bf16[4,4,256,256]{3,2,1,0:T(8,128)(2,1)} %param.3) | copy-start | bytes 6291460
  7.2 38.3 %all-gather.3.cloned.1.call-start = ((), (), s32[]{:S(2)}) async-start(), calls=%async_computation.4 | async-start | bytes 1310720 | tf_op jit(solution)/shard_map/all_gather | solution.py:27
  27.6 12.2 %all-to-all-start = ((bf16[2,8,128,64]{2,3,0,1:T(8,128)(2,1)}), bf16[2,8,128,64]{2,3,0,1:T(8,128)(2,1)S(1)}, u32[]{:S(2)}, u32[]{:S(2)}) async-start(bf16[2,8,128,64]{2,3,0,1:T(8,128)(2,1)} %copy.18), calls=%async_computation | async-start | bytes 524288 | tf_op jit(solution)/shard_map/all_to_all | solution.py:24
  33.0 60.5 %reduce-scatter.5.cloned.1.call-start = ((), (), s32[]{:S(2)}) async-start(), calls=%async_computation.3 | async-start | bytes 2621440 | tf_op jit(solution)/shard_map/reduce_scatter | solution.py:37
  45.5 1.4 %copy-start.1 = (f32[512,256]{1,0:T(8,128)S(1)}, f32[512,256]{1,0:T(8,128)}, u32[]{:S(2)}) copy-start(f32[512,256]{1,0:T(8,128)} %copy.24) | copy-start | bytes 1572868
  49.7 67.3 %reduce-scatter.7.cloned.1.call-start = ((), (), s32[]{:S(2)}) async-start(), calls=%async_computation.5 | async-start | bytes 655360
Sparse Core Ops, SparseCore 0:
  27.0 18.4 all-gather.2
  49.8 43.6 reduce-scatter.4
  96.2 20.8 reduce-scatter.6
